TPU v7x, 256 devices: a whole 4x4x8 slice. The times are simulated.
256 devices in a mesh: psg: 128 (over y, z, x), qry: 2 (over core).
Axes of the slice: x: 4, y: 4, z: 8, core: 2. Of those that a mesh axis runs over, the one named last changes fastest.
Arguments:
- queries: bfloat16 [2048, 32, 128], P(('psg', 'qry')), may hold values from -0.59765625 to 0.59765625
- cand_shard: int32 [2048, 256, 1], P(('psg', 'qry')), may hold values from 0 to 255; in each aligned block of 256 rows (0 to 255, 256 to 511, ..., all dimensions but the last counted through in order) at most 2 rows name the same one
- cand_local: int32 [2048, 256], P(('psg', 'qry')), may hold values from 0 to 63
- passages: bfloat16 [16384, 70, 128], P(('psg', 'qry')), may hold values from -0.59765625 to 0.59765625
- lengths: int32 [16384], P(('psg', 'qry')), may hold values from 8 to 70
Outputs:
- scores: float32 [2048, 256], P(('psg', 'qry'))
Inputs may be any that keep to these rules, and one draw needn't show every extreme that they name: `cand_shard`: among the 256 candidates of one query no device is named more than 2 times, and some query names some device exactly 2 times; some devices hold far more candidates than others.
All inputs are finite; a program needn't handle non-finite values.
Results may differ from a plain program's by a relative error of at most 0.0003.
Values may be sent and summed in bfloat16 or wider, within the bound.
A program may use at most 128 MiB of HBM per device.

v0:
```python
import jax
import jax.numpy as jnp
from jax import lax
from jax.sharding import PartitionSpec as P


def select_tiles(passage_row, passages, lengths):
    store_rows = passages.shape[0]
    token_slots = passages.shape[1]
    feature_dim = passages.shape[2]
    row_ids = jnp.arange(store_rows, dtype=jnp.int32)
    match_table = passage_row[..., None] == row_ids
    selector = match_table.astype(jnp.bfloat16)
    flat_store = passages.reshape(store_rows, token_slots * feature_dim)
    picked = jnp.dot(
        selector.reshape(-1, store_rows), flat_store, preferred_element_type=jnp.float32
    ).astype(jnp.bfloat16)
    picked = picked.reshape(passage_row.shape + (token_slots, feature_dim))
    token_counts = jnp.sum(jnp.where(match_table, lengths, 0), axis=-1)
    return (picked, token_counts)


def padded_block(query_matrix_rows, slot_lists, passages, lengths):
    passage_row = jnp.maximum(slot_lists, 0)
    passage_tile_block, token_counts = select_tiles(passage_row, passages, lengths)
    token_similarity = jnp.einsum(
        "ajs,aeks->aejk", query_matrix_rows, passage_tile_block, preferred_element_type=jnp.float32
    )
    positions = jnp.arange(passage_tile_block.shape[2], dtype=jnp.int32)
    valid_tokens = positions[None, None, None, :] < token_counts[:, :, None, None]
    maxsim_sum = jnp.sum(jnp.max(jnp.where(valid_tokens, token_similarity, -1e30), axis=3), axis=2)
    return jnp.where(slot_lists >= 0, maxsim_sum, 0.0)


def score_rows(query_matrix_rows, slot_lists, passages, lengths):
    row_count, capacity = slot_lists.shape
    block_rows = max(1, 512 // capacity)
    block_count = row_count // block_rows

    def tile_scores(tiles):
        return padded_block(tiles[0], tiles[1], passages, lengths)

    tiled = lax.map(
        tile_scores,
        (
            query_matrix_rows.reshape(
                block_count, block_rows, query_matrix_rows.shape[1], query_matrix_rows.shape[2]
            ),
            slot_lists.reshape(block_count, block_rows, capacity),
        ),
    )
    return tiled.reshape(row_count, capacity)


def body(queries, cand_shard, cand_local, passages, lengths):
    local_queries, pool_depth = cand_local.shape
    psg_count = lax.axis_size("psg")
    core_count = lax.axis_size("qry")
    devices_all = psg_count * core_count
    capacity = 2 * pool_depth // devices_all
    owner_device = cand_shard[:, :, 0]
    same_owner = owner_device[:, :, None] == owner_device[:, None, :]
    positions = jnp.arange(pool_depth, dtype=jnp.int32)
    before = positions[None, :] < positions[:, None]
    slot_rank = jnp.sum((same_owner & before[None]).astype(jnp.int32), axis=2)
    query_row = jnp.broadcast_to(
        jnp.arange(local_queries, dtype=jnp.int32)[:, None], owner_device.shape
    )
    outgoing = jnp.full((devices_all, local_queries, capacity), -1, jnp.int32)
    outgoing = outgoing.at[owner_device, query_row, slot_rank].set(cand_local)
    outgoing = outgoing.reshape(psg_count, core_count, local_queries, capacity)
    arrived = lax.all_to_all(
        lax.all_to_all(outgoing, "psg", split_axis=0, concat_axis=0, tiled=True),
        "qry",
        split_axis=1,
        concat_axis=1,
        tiled=True,
    )
    flat_lists = arrived.reshape(devices_all * local_queries, capacity)
    rescored_output = score_rows(
        lax.all_gather(queries, ("psg", "qry"), axis=0, tiled=True), flat_lists, passages, lengths
    )
    rescored_output = rescored_output.reshape(psg_count, core_count, local_queries, capacity)
    returned = lax.all_to_all(
        lax.all_to_all(rescored_output, "psg", split_axis=0, concat_axis=0, tiled=True),
        "qry",
        split_axis=1,
        concat_axis=1,
        tiled=True,
    )
    returned = returned.reshape(devices_all, local_queries, capacity)
    return returned[owner_device, query_row, slot_rank]


def solution(mesh):
    in_specs = (
        P(("psg", "qry"), None, None),
        P(("psg", "qry"), None, None),
        P(("psg", "qry"), None),
        P(("psg", "qry"), None, None),
        P(("psg", "qry")),
    )
    out_specs = P(("psg", "qry"), None)
    return jax.shard_map(body, mesh=mesh, in_specs=in_specs, out_specs=out_specs, check_vma=False)
```

profile of v0, /device:TPU:2, one launch (start us, length us, event | category | flops | bytes accessed | tf_op | source)
XLA Modules:
  0.0 456.3 jit_solution(17107520104302092391)
XLA Ops:
  6.5 0.7 all-gather.2.cloned.1.call-update
  7.3 0.7 copy.79
  8.0 0.8 convert_reduce_fusion
  8.8 0.7 or_bitcast_fusion
  9.5 0.7 multiply_reduce_fusion
  10.2 0.7 and_reduce_fusion
  11.0 0.7 copy.65
  11.7 8.1 %scatter_custom_fusion = s32[4096]{0:T(1024)S(1)} fusion(s32[2048]{0:T(1024)S(1)} %bitcast.56, s32[2048]{0:T(1024)S(1)} %bitcast.57, s32[]{:T(128)} %constant.7.clone.1), kind=kCustom, calls=%fused_computation.26 | custom fusion | bytes 16388
  19.9 0.8 copy.48
  20.7 15.4 %all-to-all-start = ((s32[128,2,8,2]{2,1,3,0:T(2,128)}), s32[128,2,8,2]{2,1,3,0:T(2,128)S(1)}, u32[]{:S(2)}, u32[]{:S(2)}) async-start(s32[128,2,8,2]{2,1,3,0:T(2,128)} %copy.48), calls=%async_computation | async-start | bytes 524288 | tf_op jit(solution)/shard_map/all_to_all | solution.py:73
  36.1 2.0 copy.52
  38.1 12.4 %all-to-all-done = s32[128,2,8,2]{2,1,3,0:T(2,128)S(1)} async-done(((s32[128,2,8,2]{2,1,3,0:T(2,128)}), s32[128,2,8,2]{2,1,3,0:T(2,128)S(1)}, u32[]{:S(2)}, u32[]{:S(2)}) %all-to-all-start) | async-done | bytes 16416 | tf_op jit(solution)/shard_map/all_to_all | solution.py:73
  50.6 3.7 all_to_all.20
  54.5 0.4 reshape_reshape.6
  54.8 84.4 %all-gather.2.cloned.1.call-done = bf16[2048,32,128]{2,1,0:T(8,128)(2,1)} async-done(((bf16[8,32,128]{2,1,0:T(8,128)(2,1)}), bf16[2048,32,128]{2,1,0:T(8,128)(2,1)}) %all-gather.2.cloned.1.call-update) | async-done | bytes 16777232 | tf_op jit(solution)/shard_map/all_gather | solution.py:81
  139.3 267.0 %while.10 = (s32[]{:T(128)}, f32[8,256,2]{1,0,2:T(8,128)S(1)}, s32[8,256,2]{1,0,2:T(8,128)S(1)}, s32[64]{0:T(128)}, bf16[64,70,128]{2,1,0:T(8,128)(2,1)S(1)}, /*...) while((s32[]{:T(128)}, f32[8,256,2]{1,0,2:T(8,128)S(1)}, ...), condition=%wide.region_6.7_spmd, body=%wide.region_2.6_spmd.sunk | while | flops 887852544 | bytes 40462212 | solution.py:43
  139.6 6.1 %convolution_convert_fusion.2 = bf16[512,8960]{1,0:T(8,128)(2,1)} fusion(bf16[8,8,70,128]{3,2,1,0:T(8,128)(2,1)S(1)} %bitcast.51, s32[512]{0:T(512)S(1)} %max.20), kind=kOutput, calls=%fused_computation.2.clone.1 | convolution fusion | flops 591822848 | bytes 10323968 | tf_op jit(solution)/shard_map/while/body/eval_jaxpr/dot_general | solution.py:15
  145.7 14.4 %reshape.98 = bf16[256,2,70,128]{3,2,1,0:T(8,128)(2,1)} reshape(bf16[512,8960]{1,0:T(8,128)(2,1)} %convolution_convert_fusion.2) | data formatting | bytes 18350080 | tf_op jit(solution)/shard_map/while/body/eval_jaxpr/reshape | solution.py:18
  160.7 11.5 %select_reduce_fusion.5 = f32[256,2,32]{2,1,0:T(2,128)S(1)} fusion(pred[256,2,70]{2,1,0:T(4,128)(4,1)S(1)} %iota_compare_fusion.8, bf16[256,2,70,128]{3,2,1,0:T(8,128)(2,1)} %reshape.98, bf16[8,256,32,128]{3,2,1,0:T(8,128)(2,1)} %get-tuple-element.149, s32[]{:T(128)} %get-tuple-element.135), kind=kOutput, calls=%fused_computation.3.clone.1 | convolution fusion | flops 295878656 | bytes 11636224 | tf_op jit(solution)/shard_map/while/body/eval_jaxpr/ajs,aeks->aejk/dot_general | solution.py:26
  173.0 6.1 %convolution_convert_fusion.2 = bf16[512,8960]{1,0:T(8,128)(2,1)} fusion(bf16[8,8,70,128]{3,2,1,0:T(8,128)(2,1)S(1)} %bitcast.51, s32[512]{0:T(512)S(1)} %max.20), kind=kOutput, calls=%fused_computation.2.clone.1 | convolution fusion | flops 591822848 | bytes 10323968 | tf_op jit(solution)/shard_map/while/body/eval_jaxpr/dot_general | solution.py:15
  179.0 14.4 %reshape.98 = bf16[256,2,70,128]{3,2,1,0:T(8,128)(2,1)} reshape(bf16[512,8960]{1,0:T(8,128)(2,1)} %convolution_convert_fusion.2) | data formatting | bytes 18350080 | tf_op jit(solution)/shard_map/while/body/eval_jaxpr/reshape | solution.py:18
  194.1 11.5 %select_reduce_fusion.5 = f32[256,2,32]{2,1,0:T(2,128)S(1)} fusion(pred[256,2,70]{2,1,0:T(4,128)(4,1)S(1)} %iota_compare_fusion.8, bf16[256,2,70,128]{3,2,1,0:T(8,128)(2,1)} %reshape.98, bf16[8,256,32,128]{3,2,1,0:T(8,128)(2,1)} %get-tuple-element.149, s32[]{:T(128)} %get-tuple-element.135), kind=kOutput, calls=%fused_computation.3.clone.1 | convolution fusion | flops 295878656 | bytes 11636224 | tf_op jit(solution)/shard_map/while/body/eval_jaxpr/ajs,aeks->aejk/dot_general | solution.py:26
  206.4 6.1 %convolution_convert_fusion.2 = bf16[512,8960]{1,0:T(8,128)(2,1)} fusion(bf16[8,8,70,128]{3,2,1,0:T(8,128)(2,1)S(1)} %bitcast.51, s32[512]{0:T(512)S(1)} %max.20), kind=kOutput, calls=%fused_computation.2.clone.1 | convolution fusion | flops 591822848 | bytes 10323968 | tf_op jit(solution)/shard_map/while/body/eval_jaxpr/dot_general | solution.py:15
  212.4 14.4 %reshape.98 = bf16[256,2,70,128]{3,2,1,0:T(8,128)(2,1)} reshape(bf16[512,8960]{1,0:T(8,128)(2,1)} %convolution_convert_fusion.2) | data formatting | bytes 18350080 | tf_op jit(solution)/shard_map/while/body/eval_jaxpr/reshape | solution.py:18
  227.4 11.5 %select_reduce_fusion.5 = f32[256,2,32]{2,1,0:T(2,128)S(1)} fusion(pred[256,2,70]{2,1,0:T(4,128)(4,1)S(1)} %iota_compare_fusion.8, bf16[256,2,70,128]{3,2,1,0:T(8,128)(2,1)} %reshape.98, bf16[8,256,32,128]{3,2,1,0:T(8,128)(2,1)} %get-tuple-element.149, s32[]{:T(128)} %get-tuple-element.135), kind=kOutput, calls=%fused_computation.3.clone.1 | convolution fusion | flops 295878656 | bytes 11636224 | tf_op jit(solution)/shard_map/while/body/eval_jaxpr/ajs,aeks->aejk/dot_general | solution.py:26
  239.7 6.1 %convolution_convert_fusion.2 = bf16[512,8960]{1,0:T(8,128)(2,1)} fusion(bf16[8,8,70,128]{3,2,1,0:T(8,128)(2,1)S(1)} %bitcast.51, s32[512]{0:T(512)S(1)} %max.20), kind=kOutput, calls=%fused_computation.2.clone.1 | convolution fusion | flops 591822848 | bytes 10323968 | tf_op jit(solution)/shard_map/while/body/eval_jaxpr/dot_general | solution.py:15
  245.8 14.4 %reshape.98 = bf16[256,2,70,128]{3,2,1,0:T(8,128)(2,1)} reshape(bf16[512,8960]{1,0:T(8,128)(2,1)} %convolution_convert_fusion.2) | data formatting | bytes 18350080 | tf_op jit(solution)/shard_map/while/body/eval_jaxpr/reshape | solution.py:18
  260.8 11.5 %select_reduce_fusion.5 = f32[256,2,32]{2,1,0:T(2,128)S(1)} fusion(pred[256,2,70]{2,1,0:T(4,128)(4,1)S(1)} %iota_compare_fusion.8, bf16[256,2,70,128]{3,2,1,0:T(8,128)(2,1)} %reshape.98, bf16[8,256,32,128]{3,2,1,0:T(8,128)(2,1)} %get-tuple-element.149, s32[]{:T(128)} %get-tuple-element.135), kind=kOutput, calls=%fused_computation.3.clone.1 | convolution fusion | flops 295878656 | bytes 11636224 | tf_op jit(solution)/shard_map/while/body/eval_jaxpr/ajs,aeks->aejk/dot_general | solution.py:26
  273.1 6.1 %convolution_convert_fusion.2 = bf16[512,8960]{1,0:T(8,128)(2,1)} fusion(bf16[8,8,70,128]{3,2,1,0:T(8,128)(2,1)S(1)} %bitcast.51, s32[512]{0:T(512)S(1)} %max.20), kind=kOutput, calls=%fused_computation.2.clone.1 | convolution fusion | flops 591822848 | bytes 10323968 | tf_op jit(solution)/shard_map/while/body/eval_jaxpr/dot_general | solution.py:15
  279.2 14.4 %reshape.98 = bf16[256,2,70,128]{3,2,1,0:T(8,128)(2,1)} reshape(bf16[512,8960]{1,0:T(8,128)(2,1)} %convolution_convert_fusion.2) | data formatting | bytes 18350080 | tf_op jit(solution)/shard_map/while/body/eval_jaxpr/reshape | solution.py:18
  294.2 11.5 %select_reduce_fusion.5 = f32[256,2,32]{2,1,0:T(2,128)S(1)} fusion(pred[256,2,70]{2,1,0:T(4,128)(4,1)S(1)} %iota_compare_fusion.8, bf16[256,2,70,128]{3,2,1,0:T(8,128)(2,1)} %reshape.98, bf16[8,256,32,128]{3,2,1,0:T(8,128)(2,1)} %get-tuple-element.149, s32[]{:T(128)} %get-tuple-element.135), kind=kOutput, calls=%fused_computation.3.clone.1 | convolution fusion | flops 295878656 | bytes 11636224 | tf_op jit(solution)/shard_map/while/body/eval_jaxpr/ajs,aeks->aejk/dot_general | solution.py:26
  306.5 6.1 %convolution_convert_fusion.2 = bf16[512,8960]{1,0:T(8,128)(2,1)} fusion(bf16[8,8,70,128]{3,2,1,0:T(8,128)(2,1)S(1)} %bitcast.51, s32[512]{0:T(512)S(1)} %max.20), kind=kOutput, calls=%fused_computation.2.clone.1 | convolution fusion | flops 591822848 | bytes 10323968 | tf_op jit(solution)/shard_map/while/body/eval_jaxpr/dot_general | solution.py:15
  312.6 14.4 %reshape.98 = bf16[256,2,70,128]{3,2,1,0:T(8,128)(2,1)} reshape(bf16[512,8960]{1,0:T(8,128)(2,1)} %convolution_convert_fusion.2) | data formatting | bytes 18350080 | tf_op jit(solution)/shard_map/while/body/eval_jaxpr/reshape | solution.py:18
  327.6 11.5 %select_reduce_fusion.5 = f32[256,2,32]{2,1,0:T(2,128)S(1)} fusion(pred[256,2,70]{2,1,0:T(4,128)(4,1)S(1)} %iota_compare_fusion.8, bf16[256,2,70,128]{3,2,1,0:T(8,128)(2,1)} %reshape.98, bf16[8,256,32,128]{3,2,1,0:T(8,128)(2,1)} %get-tuple-element.149, s32[]{:T(128)} %get-tuple-element.135), kind=kOutput, calls=%fused_computation.3.clone.1 | convolution fusion | flops 295878656 | bytes 11636224 | tf_op jit(solution)/shard_map/while/body/eval_jaxpr/ajs,aeks->aejk/dot_general | solution.py:26
  339.9 6.1 %convolution_convert_fusion.2 = bf16[512,8960]{1,0:T(8,128)(2,1)} fusion(bf16[8,8,70,128]{3,2,1,0:T(8,128)(2,1)S(1)} %bitcast.51, s32[512]{0:T(512)S(1)} %max.20), kind=kOutput, calls=%fused_computation.2.clone.1 | convolution fusion | flops 591822848 | bytes 10323968 | tf_op jit(solution)/shard_map/while/body/eval_jaxpr/dot_general | solution.py:15
  345.9 14.4 %reshape.98 = bf16[256,2,70,128]{3,2,1,0:T(8,128)(2,1)} reshape(bf16[512,8960]{1,0:T(8,128)(2,1)} %convolution_convert_fusion.2) | data formatting | bytes 18350080 | tf_op jit(solution)/shard_map/while/body/eval_jaxpr/reshape | solution.py:18
  360.9 11.5 %select_reduce_fusion.5 = f32[256,2,32]{2,1,0:T(2,128)S(1)} fusion(pred[256,2,70]{2,1,0:T(4,128)(4,1)S(1)} %iota_compare_fusion.8, bf16[256,2,70,128]{3,2,1,0:T(8,128)(2,1)} %reshape.98, bf16[8,256,32,128]{3,2,1,0:T(8,128)(2,1)} %get-tuple-element.149, s32[]{:T(128)} %get-tuple-element.135), kind=kOutput, calls=%fused_computation.3.clone.1 | convolution fusion | flops 295878656 | bytes 11636224 | tf_op jit(solution)/shard_map/while/body/eval_jaxpr/ajs,aeks->aejk/dot_general | solution.py:26
  373.2 6.1 %convolution_convert_fusion.2 = bf16[512,8960]{1,0:T(8,128)(2,1)} fusion(bf16[8,8,70,128]{3,2,1,0:T(8,128)(2,1)S(1)} %bitcast.51, s32[512]{0:T(512)S(1)} %max.20), kind=kOutput, calls=%fused_computation.2.clone.1 | convolution fusion | flops 591822848 | bytes 10323968 | tf_op jit(solution)/shard_map/while/body/eval_jaxpr/dot_general | solution.py:15
  379.3 14.4 %reshape.98 = bf16[256,2,70,128]{3,2,1,0:T(8,128)(2,1)} reshape(bf16[512,8960]{1,0:T(8,128)(2,1)} %convolution_convert_fusion.2) | data formatting | bytes 18350080 | tf_op jit(solution)/shard_map/while/body/eval_jaxpr/reshape | solution.py:18
  394.3 11.5 %select_reduce_fusion.5 = f32[256,2,32]{2,1,0:T(2,128)S(1)} fusion(pred[256,2,70]{2,1,0:T(4,128)(4,1)S(1)} %iota_compare_fusion.8, bf16[256,2,70,128]{3,2,1,0:T(8,128)(2,1)} %reshape.98, bf16[8,256,32,128]{3,2,1,0:T(8,128)(2,1)} %get-tuple-element.149, s32[]{:T(128)} %get-tuple-element.135), kind=kOutput, calls=%fused_computation.3.clone.1 | convolution fusion | flops 295878656 | bytes 11636224 | tf_op jit(solution)/shard_map/while/body/eval_jaxpr/ajs,aeks->aejk/dot_general | solution.py:26
  406.3 0.4 reshape_reshape.7
  406.7 0.8 copy.54
  407.5 9.7 %all-to-all-start.2 = ((f32[128,2,8,2]{2,1,3,0:T(2,128)}), f32[128,2,8,2]{2,1,3,0:T(2,128)S(1)}, u32[]{:S(2)}, u32[]{:S(2)}) async-start(f32[128,2,8,2]{2,1,3,0:T(2,128)} %copy.54), calls=%async_computation.2 | async-start | bytes 524288 | tf_op jit(solution)/shard_map/all_to_all | solution.py:85
  417.3 14.2 %all-to-all-done.2 = f32[128,2,8,2]{2,1,3,0:T(2,128)S(1)} async-done(((f32[128,2,8,2]{2,1,3,0:T(2,128)}), f32[128,2,8,2]{2,1,3,0:T(2,128)S(1)}, u32[]{:S(2)}, u32[]{:S(2)}) %all-to-all-start.2) | async-done | bytes 16416 | tf_op jit(solution)/shard_map/all_to_all | solution.py:85
  431.6 3.7 all_to_all.21
  435.3 0.5 copy.56
  435.8 13.0 %gather_fusion = f32[2048]{0:T(1024)S(1)} fusion(f32[256,8,2]{2,1,0:T(8,128)S(1)} %bitcast.50, s32[2048]{0:T(1024)S(1)} %bitcast.49), kind=kCustom, calls=%fused_computation | custom fusion | bytes 40960 | tf_op jit(solution)/shard_map/gather | solution.py:92
  448.9 0.6 reshape.85
  (124 shorter events, 11.3 us)
Async XLA Ops:
  6.5 132.8 %all-gather.2.cloned.1.call-start = ((), (), s32[]{:S(2)}) async-start(), calls=%async_computation.4 | async-start | bytes 16842752 | tf_op jit(solution)/shard_map/all_gather | solution.py:81
  20.7 29.8 %all-to-all-start = ((s32[128,2,8,2]{2,1,3,0:T(2,128)}), s32[128,2,8,2]{2,1,3,0:T(2,128)S(1)}, u32[]{:S(2)}, u32[]{:S(2)}) async-start(s32[128,2,8,2]{2,1,3,0:T(2,128)} %copy.48), calls=%async_computation | async-start | bytes 524288 | tf_op jit(solution)/shard_map/all_to_all | solution.py:73
  145.7 14.4 %copy-start = (s32[64]{0:T(128)S(1)}, s32[64]{0:T(128)}, u32[]{:S(2)}) copy-start(s32[64]{0:T(128)} %get-tuple-element.147) | copy-start | bytes 772 | tf_op jit(solution)/shard_map/while
  179.0 14.4 %copy-start = (s32[64]{0:T(128)S(1)}, s32[64]{0:T(128)}, u32[]{:S(2)}) copy-start(s32[64]{0:T(128)} %get-tuple-element.147) | copy-start | bytes 772 | tf_op jit(solution)/shard_map/while
  212.4 14.4 %copy-start = (s32[64]{0:T(128)S(1)}, s32[64]{0:T(128)}, u32[]{:S(2)}) copy-start(s32[64]{0:T(128)} %get-tuple-element.147) | copy-start | bytes 772 | tf_op jit(solution)/shard_map/while
  245.8 14.4 %copy-start = (s32[64]{0:T(128)S(1)}, s32[64]{0:T(128)}, u32[]{:S(2)}) copy-start(s32[64]{0:T(128)} %get-tuple-element.147) | copy-start | bytes 772 | tf_op jit(solution)/shard_map/while
  279.2 14.4 %copy-start = (s32[64]{0:T(128)S(1)}, s32[64]{0:T(128)}, u32[]{:S(2)}) copy-start(s32[64]{0:T(128)} %get-tuple-element.147) | copy-start | bytes 772 | tf_op jit(solution)/shard_map/while
  312.5 14.4 %copy-start = (s32[64]{0:T(128)S(1)}, s32[64]{0:T(128)}, u32[]{:S(2)}) copy-start(s32[64]{0:T(128)} %get-tuple-element.147) | copy-start | bytes 772 | tf_op jit(solution)/shard_map/while
  345.9 14.4 %copy-start = (s32[64]{0:T(128)S(1)}, s32[64]{0:T(128)}, u32[]{:S(2)}) copy-start(s32[64]{0:T(128)} %get-tuple-element.147) | copy-start | bytes 772 | tf_op jit(solution)/shard_map/while
  379.3 14.4 %copy-start = (s32[64]{0:T(128)S(1)}, s32[64]{0:T(128)}, u32[]{:S(2)}) copy-start(s32[64]{0:T(128)} %get-tuple-element.147) | copy-start | bytes 772 | tf_op jit(solution)/shard_map/while
  407.5 24.0 %all-to-all-start.2 = ((f32[128,2,8,2]{2,1,3,0:T(2,128)}), f32[128,2,8,2]{2,1,3,0:T(2,128)S(1)}, u32[]{:S(2)}, u32[]{:S(2)}) async-start(f32[128,2,8,2]{2,1,3,0:T(2,128)} %copy.54), calls=%async_computation.2 | async-start | bytes 524288 | tf_op jit(solution)/shard_map/all_to_all | solution.py:85
Sparse Core Ops, SparseCore 0:
  10.9 128.3 all-gather.1
where the time goes:
time: 462 us; the launch traced here: 456 us
  local copies, waits for them, and re-layouts  148 us (32%)
  matrix products  140 us (30%)
  waiting for transfers between devices  112 us (24%)
  starting transfers between devices  25.2 us (5%)
  between operations  13.5 us (3%)
  other arithmetic  9.32 us (2%)
  blocking collectives  7.45 us (2%)
    reshape x8, local copies, waits for them, and re-layouts, select_tiles(): picked = picked.reshape(passage_row.shape + (token_slots, feature_dim))  115 us
    dot_general x8, matrix products, padded_block(): jnp.einsum('ajs,aeks->aejk', query_matrix_rows, passage_tile_block, prefe...  91.8 us
    all_gather x1, waiting for transfers between devices, body(): lax.all_gather(queries, ('psg', 'qry'), axis=0, tiled=True)  84.4 us
    dot_general x8, matrix products, select_tiles(): jnp.dot(selector.reshape(-1, store_rows), flat_store, preferred_element_t...  48.5 us
    all_to_all x1, starting transfers between devices, body(): lax.all_to_all(outgoing, 'psg', split_axis=0, concat_axis=0, tiled=True)  15.4 us
    all_to_all x1, waiting for transfers between devices, body(): lax.all_to_all(rescored_output, 'psg', split_axis=0, concat_axis=0, tiled...  14.2 us
    gather x2, local copies, waits for them, and re-layouts, body(): return returned[owner_device, query_row, slot_rank]  13.6 us
    all_to_all x1, waiting for transfers between devices, body(): lax.all_to_all(outgoing, 'psg', split_axis=0, concat_axis=0, tiled=True)  12.4 us
  transfers between devices with their start and end apart: 3, of which 3 were waited for; matrix products, arithmetic and copies ran while one was open for 4% of the time, Pallas kernels for 0%

commit v1 on v0

v1 whole, which is shorter than its diff:
```python
import functools
import heapq

import jax
import jax.numpy as jnp
from jax import lax
from jax.experimental import pallas as pl
from jax.experimental.pallas import tpu as pltpu
from jax.sharding import PartitionSpec as P

MESH = pl.DeviceIdType.MESH
RING = {"y": 4, "z": 8, "x": 4}
CHIPS = 128
ROWS = 80
SLOTS = 4
STREAMS = ((0, 2, "xyz"), (2, 3, "yzx"), (5, 3, "xzy"))


def offsets(n):
    out = [0]
    for k in range(1, n // 2):
        out += [k, -k]
    return out + [n // 2]


def plan():
    copies = {}
    for c, (_, nq, order) in enumerate(STREAMS):
        n1, n2, n3 = (RING[a] for a in order)
        first = [(c, 1, d, h, 0) for d in (1, -1) for h in range(1, n1 // 2 + 1)]
        for d in (1, -1):
            for h in range(1, n1 // 2 + 1):
                copies[c, 1, d, h, 0] = ([(c, 1, d, h - 1, 0)] if h > 1 else [], nq / (2 if h == n1 // 2 else 1), order[0])
            for h in range(1, n2 // 2 + 1):
                copies[c, 2, d, h, 0] = ([(c, 2, d, h - 1, 0)] if h > 1 else first, nq * n1 / (2 if h == n2 // 2 else 1), order[1])
            for h in range(1, n3 // 2 + 1):
                for j, off in enumerate(offsets(n2)):
                    if h == n3 // 2 and (j % 2 == 0) != (d == 1):
                        continue
                    if h > 1:
                        needs = [(c, 3, d, h - 1, j)]
                    elif off == 0:
                        needs = first
                    elif off == n2 // 2:
                        needs = [(c, 2, e, off, 0) for e in (1, -1)]
                    else:
                        needs = [(c, 2, -1 if off > 0 else 1, abs(off), 0)]
                    copies[c, 3, d, h, j] = (needs, nq * n1, order[2])
    waiting = {key: set(needs) for key, (needs, _, _) in copies.items()}
    free, arrivals, order = {}, [], []

    def issue(key, now):
        _, size, axis = copies[key]
        link = axis, key[2]
        free[link] = max(free.get(link, 0.0), now) + size * 0.177
        heapq.heappush(arrivals, (free[link] + 1.7, len(order), key))

    for key in copies:
        if not waiting[key]:
            issue(key, 0.0)
    while arrivals:
        now, _, key = heapq.heappop(arrivals)
        order.append((key, now))
        for other, needs in waiting.items():
            if key in needs:
                needs.discard(key)
                if not needs:
                    issue(other, now)
    return copies, order


def spread_kernel(compute, q_ref, tab_ref, pp_ref, out_ref, ga, gb, gc, pp, tabv, tabs, best, total, got,
                  send, recv, aux, far):
    me, core = lax.axis_index("psg"), lax.axis_index("qry")
    m = {"x": lax.rem(me, 4), "z": lax.rem(me // 4, 8), "y": me // 32}
    gathered = (ga, gb, gc)
    copies, order = plan()
    number = {key: i for i, key in enumerate(copies)}

    def chip(axis, d):
        at = dict(m)
        at[axis] = lax.rem(m[axis] + (d + RING[axis]), RING[axis])
        return (at["y"] * 8 + at["z"]) * 4 + at["x"]

    def piece(key, sent):
        c, phase, d, h, j = key
        _, nq, axes = STREAMS[c]
        n1, n2, n3 = (RING[a] for a in axes)
        g, n, axis = gathered[c], (n1, n2, n3)[phase - 1], axes[phase - 1]
        unit = lax.rem(m[axis] + (n - d * (h - 1 if sent else h)), n)
        half = h == n // 2
        m1, m2, m3 = (m[a] for a in axes)
        if phase == 1:
            some = (pl.ds(0, nq // 2) if d == 1 else pl.ds(nq // 2, nq - nq // 2)) if half else pl.ds(0, nq)
            return g.at[m3, m2, unit, some]
        if phase == 2:
            some = pl.ds(0 if d == 1 else n1 // 2, n1 // 2) if half else pl.ds(0, n1)
            return g.at[m3, unit, some]
        return g.at[unit, lax.rem(m2 + (offsets(n2)[j] + n2), n2)]

    def remote(key, sent):
        c, phase, d, h, _ = key
        ref = piece(key, sent)
        source = ref
        if phase == 1 and h == 1 and sent:
            q0, nq, _ = STREAMS[c]
            source = q_ref.at[pl.ds(q0, nq)]
        return pltpu.make_async_remote_copy(
            src_ref=source, dst_ref=ref, send_sem=send.at[number[key]], recv_sem=recv.at[number[key]],
            device_id=(chip(STREAMS[c][2][phase - 1], d), core), device_id_type=MESH)

    waiting = {key: set(needs) for key, (needs, _, _) in copies.items()}
    for key in copies:
        if not waiting[key]:
            remote(key, True).start()

    stay = []
    for c, (q0, nq, axes) in enumerate(STREAMS):
        m1, m2, m3 = (m[a] for a in axes)
        stay.append(pltpu.make_async_copy(q_ref.at[pl.ds(q0, nq)], gathered[c].at[m3, m2, m1], aux.at[c]))
    stay.append(pltpu.make_async_copy(pp_ref, pp.at[pl.ds(core * 64, 64)], aux.at[3]))
    stay.append(pltpu.make_async_copy(tab_ref.at[pl.ds(me, 1)], tabv.at[pl.ds(me, 1)], aux.at[4]))
    for copy in stay:
        copy.start()

    def to_all(source, target, s, r):
        def one(k, _):
            other = lax.rem(me + k, CHIPS)
            pltpu.make_async_remote_copy(
                src_ref=source(other), dst_ref=target.at[pl.ds(me, 1)], send_sem=s, recv_sem=r,
                device_id=(other, core), device_id_type=MESH).start()
            return 0
        lax.fori_loop(1, CHIPS, one, 0)

    def all_done(ref, sem):
        rows = ref.at[pl.ds(0, CHIPS - 1)]
        pltpu.make_async_copy(rows, rows, sem).wait()

    to_all(lambda other: tab_ref.at[pl.ds(other, 1)], tabv, far.at[0], far.at[1])
    partner = pltpu.make_async_remote_copy(
        src_ref=pp_ref, dst_ref=pp.at[pl.ds(core * 64, 64)], send_sem=far.at[2], recv_sem=far.at[3],
        device_id=(me, 1 - core), device_id_type=MESH)
    partner.start()
    for copy in stay:
        copy.wait()

    lane = lax.broadcasted_iota(jnp.int32, (8, 128), 1)
    zero = jnp.zeros((32, 128), jnp.bfloat16)

    def score(c, y, z, u):
        line = y * 8 + z
        _, _, axes = STREAMS[c]
        q = STREAMS[c][0] + u
        at = {"y": y, "z": z}
        tiles = []
        for x in range(4):
            at["x"] = x
            tiles.append(gathered[c][at[axes[2]], at[axes[1]], at[axes[0]], u])
        w = jnp.concatenate(
            [jnp.concatenate([t, zero] if x % 2 == 0 else [zero, t], 1) for x, t in enumerate(tiles)], 0)
        sides = []
        for x in (0, 1):
            sides.append(jnp.concatenate(
                [pp[tabs[line * 4 + x + 2 * h, q * SLOTS + s]] for s in range(SLOTS) for h in range(2)], 0))
        o = lax.dot_general(jnp.concatenate(sides, 1), w, (((1,), (1,)), ((), ())), preferred_element_type=jnp.float32)
        for s in range(SLOTS):
            pair = [jnp.max(o[(2 * s + h) * ROWS:(2 * s + h + 1) * ROWS].reshape(ROWS // 8, 8, 128), axis=0) for h in range(2)]
            top = jnp.max(jnp.where(lane < 64, pair[0], pair[1]), axis=0, keepdims=True)
            best[q * SLOTS + s, pl.ds(line, 1), :] = top

    def around(axis, k):
        return lax.rem(m[axis] + (k + RING[axis]), RING[axis])

    def part(i, n):
        return lax.rem(i, n), i // n

    def blocks():
        out = []
        all1 = [key for key in copies if key[0] == 0 and key[1] < 3]

        def own0(i):
            u, y = part(i, 2)
            score(0, y, m["z"], u)
        out.append((all1, 8, own0))
        for h in range(1, 5):
            needs = [key for key in copies if key[0] == 0 and key[1] == 3 and key[3] == h]

            def far0(i, h=h):
                u, i = part(i, 2)
                y, sign = part(i, 4)
                score(0, y, lax.rem(m["z"] + 8 + h - 2 * h * sign, 8), u)
            out.append((needs, 16 if h < 4 else 8, far0))
        all2 = [key for key in copies if key[0] == 2 and key[1] < 3]

        def own2(i):
            u, z = part(i, 3)
            score(2, m["y"], z, u)
        out.append((all2, 24, own2))
        offs = offsets(8)
        for j in range(0, 8, 2):
            def hop2(i, j=j):
                u, i = part(i, 3)
                which, sign = part(i, 2)
                z = lax.rem(m["z"] + 8 + jnp.where(which == 0, offs[j], offs[j + 1]), 8)
                score(2, lax.rem(m["y"] + 4 + 1 - 2 * sign, 4), z, u)
            out.append(([key for key in copies if key[0] == 2 and key[1:2] == (3,) and key[3] == 1 and key[4] in (j, j + 1)], 12, hop2))
        for j in range(0, 8, 4):
            def last2(i, j=j):
                u, w = part(i, 3)
                off = jnp.where(w < 2, jnp.where(w == 0, offs[j], offs[j + 1]), jnp.where(w == 2, offs[j + 2], offs[j + 3]))
                score(2, around("y", 2), lax.rem(m["z"] + 8 + off, 8), u)
            out.append(([key for key in copies if key[0] == 2 and key[1] == 3 and key[3] == 2 and j <= key[4] < j + 4], 12, last2))
        for j in range(8):
            def line1(i, j=j):
                u, y = part(i, 3)
                score(1, y, lax.rem(m["z"] + 8 + offs[j], 8), u)
            needs = [key for key in copies if key[0] == 1 and key[1] == 3 and key[4] == j]
            needs += [key for key in copies if key[0] == 1 and key[1] < 3]
            out.append((needs, 12, line1))
        return out

    todo = [(set(needs), n, f) for needs, n, f in blocks()]
    ready, started, clock = [], False, 0.0

    def run(job):
        _, n, f = job
        unroll = 4

        def some(i, _):
            for k in range(unroll):
                f(i * unroll + k)
            return 0
        lax.fori_loop(0, n // unroll, some, 0)

    for key, now in order:
        while compute and ready and clock < now:
            if not started:
                all_done(tabv, far.at[1])
                partner.wait_recv()
                copy = pltpu.make_async_copy(tabv, tabs, aux.at[5])
                copy.start()
                copy.wait()
                started = True
            job = ready.pop(0)
            run(job)
            clock = max(clock, 0.0) + 0.13 * job[1]
        clock = max(clock, now)
        remote(key, False).wait_recv()
        for other, needs in waiting.items():
            if key in needs:
                needs.discard(key)
                if not needs:
                    remote(other, True).start()
        for job in todo:
            if key in job[0]:
                job[0].discard(key)
                if not job[0]:
                    ready.append(job)
    if not started:
        all_done(tabv, far.at[1])
        partner.wait_recv()
        copy = pltpu.make_async_copy(tabv, tabs, aux.at[5])
        copy.start()
        copy.wait()
    if compute:
        for job in ready:
            run(job)
    lanes = lax.broadcasted_iota(jnp.int32, (32, 128), 1) % 32
    sums = jnp.zeros((32, 128), jnp.float32)
    for v in range(32):
        s = best[v]
        for step in (16, 8, 4, 2, 1):
            s = s + pltpu.roll(s, 128 - step, 1)
        sums = jnp.where(lanes == v, pltpu.roll(s, v, 1) if v else s, sums)
    total[...] = sums
    to_all(lambda other: total.at[pl.ds(other // 4, 1)], got, far.at[4], far.at[5])
    mine = pltpu.make_async_copy(total.at[pl.ds(me // 4, 1)], got.at[pl.ds(me, 1)], aux.at[6])
    mine.start()
    for key in copies:
        remote(key, True).wait_send()
    partner.wait_send()
    all_done(tabv, far.at[0])
    mine.wait()
    all_done(got, far.at[4])
    all_done(got, far.at[5])
    out_ref[...] = got[...]


def spread(q, tab, passages, compute=True):
    n = len(plan()[0])
    vmem = pl.BlockSpec(memory_space=pltpu.VMEM)
    scratch = []
    for _, nq, axes in STREAMS:
        scratch.append(pltpu.VMEM((RING[axes[2]], RING[axes[1]], RING[axes[0]], nq, 32, 128), jnp.bfloat16))
    scratch += [
        pltpu.VMEM((128, ROWS, 128), jnp.bfloat16),
        pltpu.VMEM((CHIPS, 128), jnp.int32),
        pltpu.SMEM((CHIPS, 128), jnp.int32),
        pltpu.VMEM((32, 32, 128), jnp.float32),
        pltpu.VMEM((32, 128), jnp.float32),
        pltpu.VMEM((CHIPS, 128), jnp.float32),
        pltpu.SemaphoreType.DMA((n,)),
        pltpu.SemaphoreType.DMA((n,)),
        pltpu.SemaphoreType.DMA((8,)),
        pltpu.SemaphoreType.DMA((8,)),
    ]
    return pl.pallas_call(
        functools.partial(spread_kernel, compute),
        out_shape=jax.ShapeDtypeStruct((CHIPS, 128), jnp.float32),
        in_specs=[vmem, vmem, vmem],
        out_specs=vmem,
        scratch_shapes=scratch,
        compiler_params=pltpu.CompilerParams(has_side_effects=True, vmem_limit_bytes=48 * 2**20),
        name="spread",
    )(q, tab, passages)


def matches(chip_row, upper):
    hit = lax.broadcasted_iota(jnp.int32, (CHIPS, 256), 0) == chip_row
    rank = jnp.dot(jnp.where(hit, 1.0, 0.0).astype(jnp.bfloat16), upper, preferred_element_type=jnp.float32)
    return hit, rank


def upper_ones():
    r = lax.broadcasted_iota(jnp.int32, (256, 256), 0)
    c = lax.broadcasted_iota(jnp.int32, (256, 256), 1)
    return jnp.where(r < c, 1.0, 0.0).astype(jnp.bfloat16)


def table_kernel(shard_ref, local_ref, tab_ref):
    upper = upper_ones()
    owner = shard_ref[...]
    value = ((owner & 1) * 64 + local_ref[...]).astype(jnp.float32)
    lane = lax.broadcasted_iota(jnp.int32, (CHIPS, 128), 1)
    acc = jnp.zeros((CHIPS, 128), jnp.float32)
    for q in range(8):
        hit, rank = matches(owner[q:q + 1] >> 1, upper)
        there = jnp.where(hit, value[q:q + 1], 0.0)
        for s in range(SLOTS):
            col = jnp.sum(jnp.where(rank == s, there, 0.0), axis=1, keepdims=True)
            acc = jnp.where(lane == q * SLOTS + s, col, acc)
    tab_ref[...] = acc.astype(jnp.int32)


def pick_kernel(shard_ref, got_ref, out_ref):
    x = lax.rem(lax.axis_index("psg"), 4)
    got = got_ref[...]
    mine = got
    for k in range(1, 4):
        mine = jnp.where(x == k, pltpu.roll(got, 128 - 32 * k, 1), mine)
    upper = upper_ones()
    owner = shard_ref[...]
    for q in range(8):
        hit, rank = matches(owner[q:q + 1] >> 1, upper)
        acc = jnp.zeros((CHIPS, 256), jnp.float32)
        for s in range(SLOTS):
            acc = jnp.where(rank == s, mine[:, q * SLOTS + s:q * SLOTS + s + 1], acc)
        out_ref[pl.ds(q, 1), :] = jnp.sum(jnp.where(hit, acc, 0.0), axis=0, keepdims=True)


def body(queries, cand_shard, cand_local, passages, lengths):
    owner = cand_shard[:, :, 0]
    slot = jnp.arange(ROWS, dtype=jnp.int32)
    wide = jnp.pad(passages, ((0, 0), (0, ROWS - passages.shape[1]), (0, 0)))
    tokens = jnp.where((slot[None, :] < lengths[:, None])[:, :, None], wide, passages[:, :1, :])
    vmem = pl.BlockSpec(memory_space=pltpu.VMEM)
    tab = pl.pallas_call(
        table_kernel, out_shape=jax.ShapeDtypeStruct((CHIPS, 128), jnp.int32),
        in_specs=[vmem, vmem], out_specs=vmem, name="table")(owner, cand_local)
    got = spread(queries, tab, tokens)
    return pl.pallas_call(
        pick_kernel, out_shape=jax.ShapeDtypeStruct(cand_local.shape, jnp.float32),
        in_specs=[vmem, vmem], out_specs=vmem, name="pick")(owner, got)


def solution(mesh):
    both = ("psg", "qry")
    in_specs = (P(both, None, None), P(both, None, None), P(both, None), P(both, None, None), P(both))
    return jax.shard_map(body, mesh=mesh, in_specs=in_specs, out_specs=P(both, None), check_vma=False)
```

time: 462 us -> 114 us (0.25); the launches traced: 456 us -> 113 us
  local copies, waits for them, and re-layouts: 148 us -> 4.64 us
  matrix products: 140 us -> 0 us
  waiting for transfers between devices: 112 us -> 0 us
  Pallas kernels: 0 us -> 107 us
  starting transfers between devices: 25.2 us -> 0 us
  between operations: 13.5 us -> 0.07 us
  other arithmetic: 9.32 us -> 1.74 us
  blocking collectives: 7.45 us -> 0 us
    dot_general x16 -> x0, matrix products: 140 us -> none  [the longest x8 91.8 us: padded_block(): jnp.einsum('ajs,aeks->aejk', query_matrix_rows, passage_tile_block, prefe...]
    reshape x9 -> x0, local copies, waits for them, and re-layouts: 116 us -> none  [the longest x8 115 us: select_tiles(): picked = picked.reshape(passage_row.shape + (token_slots, feature_dim))]
    pallas_call x0 -> x3, Pallas kernels: none -> 107 us  [the longest x1 102 us: spread(): pl.pallas_call(functools.partial(spread_kernel, compute), out_shape=jax.S...]
    all_gather x1 -> x0, waiting for transfers between devices: 84.4 us -> none  [body(): lax.all_gather(queries, ('psg', 'qry'), axis=0, tiled=True)]
    all_to_all x2 -> x0, waiting for transfers between devices: 26.6 us -> none  [the longest x1 14.2 us: body(): lax.all_to_all(rescored_output, 'psg', split_axis=0, concat_axis=0, tiled...]
    all_to_all x2 -> x0, starting transfers between devices: 25.2 us -> none  [the longest x1 15.4 us: body(): lax.all_to_all(outgoing, 'psg', split_axis=0, concat_axis=0, tiled=True)]
    gather x2 -> x0, local copies, waits for them, and re-layouts: 13.6 us -> none  [body(): return returned[owner_device, query_row, slot_rank]]
    all_to_all x2 -> x0, blocking collectives: 7.45 us -> none  [the longest x1 3.72 us: body(): lax.all_to_all(lax.all_to_all(outgoing, 'psg', split_axis=0, concat_axis=...]
  transfers between devices with their start and end apart: 3 -> 0, of which waited for: 3 -> 0; matrix products, arithmetic and copies ran while one was open for 4% -> 0% of each run, Pallas kernels for 0% -> 0%
where the time goes in v1:
time: 114 us; the launch traced here: 113 us
  Pallas kernels  107 us (94%)
  local copies, waits for them, and re-layouts  4.64 us (4%)
  other arithmetic  1.74 us (2%)
    pallas_call x1, Pallas kernels, spread(): pl.pallas_call(functools.partial(spread_kernel, compute), out_shape=jax.S...  102 us
    unnamed x8, local copies, waits for them, and re-layouts  3.92 us
    pallas_call x1, Pallas kernels, body(): pl.pallas_call(pick_kernel, out_shape=jax.ShapeDtypeStruct(cand_local.sha...  2.4 us

profile of v1, /device:TPU:2, one launch (start us, length us, event | category | flops | bytes accessed | tf_op | source)
XLA Modules:
  0.0 113.2 jit_solution(1397762050393577629)
XLA Ops:
  0.0 1.3 %copy.9 = s32[8,256,1]{1,0,2:T(8,128)} copy(s32[8,256,1]{1,2,0:T(1,128)} %param.6) | data formatting | bytes 16384
  1.3 0.7 iota_compare_fusion
  2.0 0.7 slice_bitcast_fusion
  2.8 2.2 %table.1.tab_ref = s32[128,128]{1,0:T(8,128)} custom-call(s32[8,256]{1,0:T(8,128)} %bitcast.5, s32[8,256]{1,0:T(8,128)} %local_ref.1), custom_call_target="tpu_custom_call" | custom-call | tf_op jit(solution)/shard_map/table/pallas_call | solution.py:367
  5.0 2.0 %copy.6 = bf16[64,70,128]{2,1,0:T(8,128)(2,1)S(1)} copy(bf16[64,70,128]{2,0,1:T(8,128)(2,1)} %param.8) | data formatting | bytes 2293760 | tf_op args[3]
  7.0 0.0 copy-start
  7.0 0.0 copy-start.2
  7.0 1.0 pad_select_fusion.pp_ref
  8.0 0.0 copy-done
  8.0 0.0 copy-done.2
  8.0 102.2 %spread.1.got_ref = f32[128,128]{1,0:T(8,128)S(1)} custom-call(bf16[8,32,128]{2,1,0:T(8,128)(2,1)S(1)} %copy-done.2, s32[128,128]{1,0:T(8,128)S(1)} %copy-done, bf16[64,80,128]{2,1,0:T(8,128)(2,1)S(1)} %pad_select_fusion.pp_ref), custom_call_target="tpu_custom_call" | custom-call | tf_op jit(solution)/shard_map/spread/pallas_call | solution.py:307
  110.2 0.0 copy-start.1
  110.2 0.6 copy-done.1
  110.8 2.4 %pick.1 = f32[8,256]{1,0:T(8,128)} custom-call(s32[8,256]{1,0:T(8,128)} %bitcast.6, f32[128,128]{1,0:T(8,128)} %copy-done.1), custom_call_target="tpu_custom_call" | custom-call | tf_op jit(solution)/shard_map/pick/pallas_call | solution.py:371
Async XLA Ops:
  7.0 1.0 copy-start
  7.0 1.0 copy-start.2
  110.2 0.6 copy-start.1
